TPU v7x, 32 devices: a whole 2x2x4 slice. The times are simulated.
32 devices in a mesh: row: 4 (over y, x), col: 8 (over z, core).
Axes of the slice: x: 2, y: 2, z: 4, core: 2. Of those that a mesh axis runs over, the one named last changes fastest.
Arguments:
- object_tiles: float32 [2, 2, 1024, 2048], P(None, None, 'row', 'col'), may hold values from -5 to 5
- probe_modes: float32 [2, 4, 128, 128], replicated, may hold values from -6 to 6
- offsets: int32 [4, 8, 3, 2], P('row', 'col'), may hold values from 0 to 192
- amplitude: float32 [4, 8, 3, 128, 128], P('row', 'col'), may hold values from 0.2 to 3
Outputs:
- object_grad: float32 [2, 2, 1024, 2048], P(None, None, 'row', 'col')
- probe_new: float32 [2, 4, 128, 128], replicated
All inputs are finite; a program needn't handle non-finite values.
Results may differ from a plain program's by a relative error of at most 0.0003.
Values sent between devices are 32-bit elements; how exact they have to be, the bound alone decides.
A program may use at most 64 MiB of HBM per device.

v0:
```python
import functools

import jax
import jax.numpy as jnp
import numpy as np
from jax import lax
from jax.experimental import pallas as pl
from jax.experimental.pallas import tpu as pltpu
from jax.sharding import PartitionSpec as P

HALO = 32
PROP = 0.002
SHIFT_AMP = 0.5
STEP_SIZE = 0.5
EPSILON = 1e-06
LANES = 128
SUB = 8
MESH = pl.DeviceIdType.MESH
F32 = jnp.float32
BF16 = jnp.bfloat16


def tables(win):
    k = np.arange(win)
    c = np.exp(-2j * np.pi * (k[:, None] * k[None, :] % win) / win) / np.sqrt(win)
    freq = (k + win // 2) % win - win // 2
    kern = np.conj(c) @ np.diag(np.exp(-1j * PROP * freq**2)) @ c
    out = []
    for m in (c, np.conj(c), kern, np.conj(kern)):
        full = np.block([[m.real, m.imag], [-m.imag, m.real]])
        high = full.astype(np.float32).astype(jnp.bfloat16)
        low = (full - high.astype(np.float64)).astype(np.float32).astype(jnp.bfloat16)
        out += [high, low]
    return np.stack(out)


FWD, INV, KER, KER_INV = 0, 1, 2, 3


def split(x):
    high = x.astype(BF16)
    return high, (x - high.astype(F32)).astype(BF16)


def dot(a, b):
    return jnp.dot(a, b, preferred_element_type=F32)


def right(x, tab, which):
    high, low = split(x)
    return dot(high, tab[2 * which]) + (
        dot(low, tab[2 * which]) + dot(high, tab[2 * which + 1])
    )


def left(x, tab, which):
    high, low = split(x)
    which = which ^ 1
    return dot(tab[2 * which], high) + (
        dot(tab[2 * which], low) + dot(tab[2 * which + 1], high)
    )


def swap(y):
    w = y.shape[0] // 2
    top = jnp.concatenate([y[:w, :w], y[w:, :w]], axis=1)
    low = jnp.concatenate([y[:w, w:], y[w:, w:]], axis=1)
    return jnp.concatenate([top, low], axis=0)


def twice(x, axis):
    return jnp.concatenate([x, x], axis=axis)


def lane(rows):
    return lax.broadcasted_iota(jnp.int32, (rows, LANES), 1)


CHANS = [(part, lay) for part in range(2) for lay in range(2)]
EVERY = slice(None)


def packed(get, first, rows):
    out = None
    for ch in range(4):
        shift = (HALO * ch - first) % LANES
        block = get(ch)
        block = pltpu.roll(block, shift, 1) if shift else block
        at = lane(rows)
        keep = (at >= HALO * ch) & (at < HALO * ch + HALO)
        out = jnp.where(keep, block, 0.0 if out is None else out)
    return out


def unpacked(block, ch, first):
    shift = (first - HALO * ch) % LANES
    return pltpu.roll(block, shift, 1) if shift else block


def send(src, dst, ssem, rsem, i, to):
    copy = pltpu.make_async_remote_copy(
        src_ref=src,
        dst_ref=dst,
        send_sem=ssem.at[i],
        recv_sem=rsem.at[i],
        device_id=to,
        device_id_type=MESH,
    )
    copy.start()
    return copy


def places(n_row, n_col):
    my_r = lax.axis_index("row")
    my_c = lax.axis_index("col")
    up = lax.rem(my_r + n_row - 1, n_row)
    down = lax.rem(my_r + 1, n_row)
    lft = lax.rem(my_c + n_col - 1, n_col)
    rgt = lax.rem(my_c + 1, n_col)
    return my_r, my_c, up, down, lft, rgt


def zones(tile):
    head, tail = pl.ds(0, HALO), pl.ds(tile - HALO, HALO)
    mid, after, body = pl.ds(HALO, tile), pl.ds(HALO + tile, HALO), pl.ds(0, tile)
    return head, tail, mid, after, body


def rows_of(p, win):
    return [[(4 * p + 2 * part + m) * win for m in range(2)] for part in range(2)]


def halo_kernel(
    sizes, obj_ref, ext, pack_l, pack_r, halo_l, halo_r, h_send, h_recv
):
    n_row, n_col = sizes
    tile = obj_ref.shape[2]
    tall = tile + 2 * HALO
    wide = tile + LANES
    my_r, my_c, up, down, lft, rgt = places(n_row, n_col)
    head, tail, mid, after, body = zones(tile)
    barrier = pltpu.get_barrier_semaphore()
    around = [(r, c) for r in (up, my_r, down) for c in (lft, my_c, rgt)]
    del around[4]
    for to in around:
        pl.semaphore_signal(barrier, inc=1, device_id=to, device_id_type=MESH)
    pack_l[...] = packed(lambda ch: obj_ref[CHANS[ch] + (EVERY, slice(0, LANES))], 0, tile)
    pack_r[...] = packed(
        lambda ch: obj_ref[CHANS[ch] + (EVERY, slice(tile - LANES, tile))], LANES - HALO, tile
    )
    pl.semaphore_wait(barrier, 8)
    halo = [
        send(obj_ref.at[:, :, tail, :], ext.at[:, :, head, body], h_send, h_recv, 0, (down, my_c)),
        send(obj_ref.at[:, :, head, :], ext.at[:, :, after, body], h_send, h_recv, 1, (up, my_c)),
        send(pack_r, halo_l.at[mid], h_send, h_recv, 2, (my_r, rgt)),
        send(pack_l, halo_r.at[mid], h_send, h_recv, 3, (my_r, lft)),
        send(pack_r.at[tail], halo_l.at[head], h_send, h_recv, 4, (down, rgt)),
        send(pack_r.at[head], halo_l.at[after], h_send, h_recv, 5, (up, rgt)),
        send(pack_l.at[tail], halo_r.at[head], h_send, h_recv, 6, (down, lft)),
        send(pack_l.at[head], halo_r.at[after], h_send, h_recv, 7, (up, lft)),
    ]
    ext[:, :, mid, body] = obj_ref[...]
    ext[:, :, pl.ds(tall, SUB), :] = jnp.zeros((2, 2, SUB, wide), F32)
    for copy in halo:
        copy.wait()
    for ch in range(4):
        near = unpacked(halo_r[...], ch, 0)
        far_side = unpacked(halo_l[...], ch, LANES - HALO)
        at = lane(tall)
        edge = jnp.where(at < HALO, near, jnp.where(at >= LANES - HALO, far_side, 0.0))
        ext[CHANS[ch] + (pl.ds(0, tall), pl.ds(tile, LANES))] = edge


def local_kernel(
    sizes, off_ref, ext, probe_ref, amp_ref, tab, acc, gprobe, winds, wave, far, factor, gobj
):
    win, scans = sizes
    wide = ext.shape[3]
    acc[...] = jnp.zeros_like(acc)
    gprobe[...] = jnp.zeros_like(gprobe)
    gobj[...] = jnp.zeros_like(gobj)

    @pl.loop(0, scans)
    def _(s):
        row = off_ref[0, 0, s, 0]
        base = pl.multiple_of(row - lax.rem(row, SUB), SUB)
        rest = lax.rem(win + SUB - lax.rem(row, SUB), win + SUB)
        shift = lax.rem(wide + HALO - off_ref[0, 0, s, 1], wide)
        o = {}
        for ch, (part, lay) in enumerate(CHANS):
            block = ext[part, lay, pl.ds(base, win + SUB), :]
            block = pltpu.roll(block, shift, 1)[:, :win]
            o[part, lay] = pltpu.roll(block, rest, 0)[:win]
            winds[s, ch] = o[part, lay]
        power = None
        for p in range(2):
            rows = []
            for m in range(2):
                pr, pi = probe_ref[0, 2 * p + m], probe_ref[1, 2 * p + m]
                rows.append(
                    jnp.concatenate(
                        [
                            pr * o[0, 0] - pi * o[1, 0],
                            pr * o[1, 0] + pi * o[0, 0],
                        ],
                        axis=1,
                    )
                )
            psi = jnp.concatenate(rows, axis=0)
            w = left(swap(right(psi, tab, KER)), tab, KER)
            wave[s, p] = w
            wr, wi = w[:win], w[win:]
            o1r, o1i = twice(o[0, 1], 1), twice(o[1, 1], 1)
            psi = jnp.concatenate([wr * o1r - wi * o1i, wr * o1i + wi * o1r], axis=0)
            psi = right(swap(left(psi, tab, FWD)), tab, FWD)
            far[s, p] = psi
            sq = psi * psi
            part_sum = (sq[:win, :win] + sq[:win, win:]) + (sq[win:, :win] + sq[win:, win:])
            power = part_sum if power is None else power + part_sum
        root = jnp.sqrt(power + SHIFT_AMP)
        factor[s] = 2.0 * (root - amp_ref[0, 0, s]) / root

    def backward(p, s):
        f = factor[s]
        g = far[s, p] * twice(twice(f, 0), 1)
        g = left(swap(right(g, tab, INV)), tab, INV)
        w = wave[s, p]
        gr, gi, wr, wi = g[:win], g[win:], w[:win], w[win:]
        re = wr * gr + wi * gi
        im = wr * gi - wi * gr
        gobj[s, 1] += re[:, :win] + re[:, win:]
        gobj[s, 3] += im[:, :win] + im[:, win:]
        o1r, o1i = twice(winds[s, 1], 1), twice(winds[s, 3], 1)
        g = jnp.concatenate([o1r * gr + o1i * gi, o1r * gi - o1i * gr], axis=0)
        g = right(swap(left(g, tab, KER_INV)), tab, KER_INV)
        o0r, o0i = winds[s, 0], winds[s, 2]
        re = im = None
        for m in range(2):
            gr, gi = g[m * win : (m + 1) * win, :win], g[m * win : (m + 1) * win, win:]
            pr, pi = probe_ref[0, 2 * p + m], probe_ref[1, 2 * p + m]
            a = pr * gr + pi * gi
            b = pr * gi - pi * gr
            re, im = (a, b) if re is None else (re + a, im + b)
            at = rows_of(p, win)
            gprobe[pl.ds(at[0][m], win)] += o0r * gr + o0i * gi
            gprobe[pl.ds(at[1][m], win)] += o0r * gi - o0i * gr
        gobj[s, 0] += re
        gobj[s, 2] += im

    @pl.loop(0, scans)
    def _(s):
        backward(0, s)

    @pl.loop(0, scans)
    def _(s):
        backward(1, s)
        row = off_ref[0, 0, s, 0]
        rest = lax.rem(row, SUB)
        base = pl.multiple_of(row - rest, SUB)
        shift = lax.rem(wide - HALO + off_ref[0, 0, s, 1], wide)
        for ch, (part, lay) in enumerate(CHANS):
            block = jnp.concatenate([gobj[s, ch], jnp.zeros((SUB, win), F32)], axis=0)
            block = pltpu.roll(block, rest, 0)
            block = jnp.concatenate([block, jnp.zeros((win + SUB, wide - win), F32)], axis=1)
            acc[part, lay, pl.ds(base, win + SUB), :] += pltpu.roll(block, shift, 1)


def sum_kernel(
    sizes,
    acc,
    gprobe,
    probe_ref,
    grad_ref,
    new_ref,
    total,
    from_top,
    from_bot,
    edge_l,
    edge_r,
    from_l,
    from_r,
    parts,
    g_send,
    g_recv,
    rs_send,
    rs_recv,
    ag_send,
    ag_recv,
):
    n_row, n_col, chunks = sizes
    n_dev = n_row * n_col
    tile, win = grad_ref.shape[2], probe_ref.shape[2]
    tall = tile + 2 * HALO
    my_r, my_c, up, down, lft, rgt = places(n_row, n_col)
    head, tail, mid, after, body = zones(tile)
    me = my_r * n_col + my_c

    def peer(k):
        other = lax.rem(me + k, n_dev)
        return other, (other // n_col, lax.rem(other, n_col))

    barrier = pltpu.get_barrier_semaphore()

    @pl.loop(1, n_dev)
    def _(k):
        pl.semaphore_signal(barrier, inc=1, device_id=peer(k)[1], device_id_type=MESH)

    tall_rows = pl.ds(0, tall)
    edge_of = lambda ch: acc[CHANS[ch] + (tall_rows, pl.ds(tile, LANES))]
    edge_r[...] = packed(edge_of, 0, tall)
    edge_l[...] = packed(edge_of, LANES - HALO, tall)
    pl.semaphore_wait(barrier, n_dev - 1)

    n_rows = gprobe.shape[0] // chunks
    piece = n_rows // n_dev

    def scatter_start(c):
        @pl.loop(1, n_dev)
        def _(k):
            other, where = peer(k)
            send(
                gprobe.at[pl.ds(pl.multiple_of(c * n_rows + other * piece, piece), piece)],
                parts.at[c, pl.ds(pl.multiple_of((k - 1) * piece, piece), piece)],
                rs_send,
                rs_recv,
                c,
                where,
            )

    mine = [
        pl.ds(pl.multiple_of(c * n_rows + me * piece, piece), piece) for c in range(chunks)
    ]

    def wait_all(sem, ref):
        pltpu.make_async_copy(ref, ref, sem).wait()

    def gather_start(c):
        wait_all(rs_recv.at[c], parts.at[c])
        value = gprobe[mine[c]]
        for k in range(n_dev - 1):
            value = value + parts[c, pl.ds(k * piece, piece)]
        total[mine[c]] = value

        @pl.loop(1, n_dev)
        def _(k):
            _, where = peer(k)
            send(total.at[mine[c]], total.at[mine[c]], ag_send, ag_recv, c, where)

    for c in range(chunks):
        scatter_start(c)
    grads = [
        send(acc.at[:, :, head, body], from_bot, g_send, g_recv, 0, (up, my_c)),
        send(acc.at[:, :, after, body], from_top, g_send, g_recv, 1, (down, my_c)),
        send(edge_r.at[mid], from_l.at[mid], g_send, g_recv, 2, (my_r, rgt)),
        send(edge_l.at[mid], from_r.at[mid], g_send, g_recv, 3, (my_r, lft)),
        send(edge_r.at[head], from_l.at[after], g_send, g_recv, 4, (up, rgt)),
        send(edge_r.at[after], from_l.at[head], g_send, g_recv, 5, (down, rgt)),
        send(edge_l.at[head], from_r.at[after], g_send, g_recv, 6, (up, lft)),
        send(edge_l.at[after], from_r.at[head], g_send, g_recv, 7, (down, lft)),
    ]
    for c in range(chunks):
        gather_start(c)
    grad_ref[...] = acc[:, :, mid, body]
    for copy in grads:
        copy.wait()
    grad_ref[:, :, head, :] += from_top[...]
    grad_ref[:, :, tail, :] += from_bot[...]
    for ref, first, cols in (
        (from_l, 0, pl.ds(0, LANES)),
        (from_r, LANES - HALO, pl.ds(tile - LANES, LANES)),
    ):
        for ch in range(4):
            at = lane(tall)
            block = unpacked(ref[...], ch, first)
            block = jnp.where((at >= first) & (at < first + HALO), block, 0.0)
            part, lay = CHANS[ch]
            grad_ref[part, lay, :, cols] += block[HALO : HALO + tile]
            grad_ref[part, lay, head, cols] += block[:HALO]
            grad_ref[part, lay, tail, cols] += block[HALO + tile :]
    for c in range(chunks):
        wait_all(ag_recv.at[c], parts.at[c])
    full = total[...]
    scale = STEP_SIZE / jnp.sqrt(jnp.sum(full * full, keepdims=True) / full.size + EPSILON)
    for p in range(2):
        for part in range(2):
            for m in range(2):
                at = rows_of(p, win)[part][m]
                new_ref[part, 2 * p + m] = (
                    probe_ref[part, 2 * p + m] - scale * total[pl.ds(at, win)]
                )
    for c in range(chunks):
        wait_all(rs_send.at[c], parts.at[c])
        wait_all(ag_send.at[c], parts.at[c])


def on_device(object_tiles, probe_modes, offsets, amplitude):
    n_row, n_col = lax.axis_size("row"), lax.axis_size("col")
    n_dev = n_row * n_col
    tile, win, scans = object_tiles.shape[2], probe_modes.shape[2], offsets.shape[2]
    tall, wide = tile + 2 * HALO, tile + LANES
    g_rows = 2 * probe_modes.shape[1] * win
    chunks = 2 if g_rows // 2 % (8 * n_dev) == 0 else 1
    piece = g_rows // chunks // n_dev
    vmem = pl.BlockSpec(memory_space=pltpu.VMEM)
    smem = pl.BlockSpec(memory_space=pltpu.SMEM)
    dma = pltpu.SemaphoreType.DMA
    side = pltpu.VMEM((tall, LANES), F32)
    wide_tile = jax.ShapeDtypeStruct((2, 2, tall + SUB, wide), F32)
    limit = 40 * 1024 * 1024
    ext = pl.pallas_call(
        functools.partial(halo_kernel, (n_row, n_col)),
        out_shape=wide_tile,
        in_specs=[vmem],
        out_specs=vmem,
        scratch_shapes=[
            pltpu.VMEM((tile, LANES), F32),
            pltpu.VMEM((tile, LANES), F32),
            side,
            side,
            dma((8,)),
            dma((8,)),
        ],
        compiler_params=pltpu.CompilerParams(
            collective_id=0, has_side_effects=True, vmem_limit_bytes=limit
        ),
    )(object_tiles)
    acc, gprobe = pl.pallas_call(
        functools.partial(local_kernel, (win, scans)),
        out_shape=(wide_tile, jax.ShapeDtypeStruct((g_rows, win), F32)),
        in_specs=[smem] + [vmem] * 4,
        out_specs=(vmem, vmem),
        scratch_shapes=[
            pltpu.VMEM((scans, 4, win, win), F32),
            pltpu.VMEM((scans, 2, 2 * win, 2 * win), F32),
            pltpu.VMEM((scans, 2, 2 * win, 2 * win), F32),
            pltpu.VMEM((scans, win, win), F32),
            pltpu.VMEM((scans, 4, win, win), F32),
        ],
        compiler_params=pltpu.CompilerParams(vmem_limit_bytes=limit),
    )(offsets, ext, probe_modes, amplitude, jnp.asarray(tables(win)))
    return pl.pallas_call(
        functools.partial(sum_kernel, (n_row, n_col, chunks)),
        out_shape=(
            jax.ShapeDtypeStruct(object_tiles.shape, F32),
            jax.ShapeDtypeStruct(probe_modes.shape, F32),
        ),
        in_specs=[vmem] * 3,
        out_specs=(vmem, vmem),
        scratch_shapes=[
            pltpu.VMEM((g_rows, win), F32),
            pltpu.VMEM((2, 2, HALO, tile), F32),
            pltpu.VMEM((2, 2, HALO, tile), F32),
            side,
            side,
            side,
            side,
            pltpu.VMEM((chunks, (n_dev - 1) * piece, win), F32),
            dma((8,)),
            dma((8,)),
            dma((chunks,)),
            dma((chunks,)),
            dma((chunks,)),
            dma((chunks,)),
        ],
        compiler_params=pltpu.CompilerParams(
            collective_id=1, has_side_effects=True, vmem_limit_bytes=limit
        ),
    )(acc, gprobe, probe_modes)


def solution(mesh):
    placed = (
        P(None, None, "row", "col"),
        P(),
        P("row", "col", None, None),
        P("row", "col", None, None, None),
    )
    return jax.shard_map(
        on_device,
        mesh=mesh,
        in_specs=placed,
        out_specs=(P(None, None, "row", "col"), P()),
        check_vma=False,
    )
```

profile of v0, /device:TPU:1, one launch (start us, length us, event | category | flops | bytes accessed | tf_op | source)
XLA Modules:
  0.0 66.7 jit_solution(11174882932304385979)
XLA Ops:
  0.6 0.0 copy-start
  0.6 0.8 %copy.7.off_ref = s32[1,1,3,2]{3,2,1,0:T(4,128)S(1)} copy(s32[1,1,3,2]{2,3,1,0:T(2,128)} %param.7) | data formatting | bytes 48 | tf_op args[2]
  1.5 0.0 copy-start.1
  1.5 1.2 %copy-done.1 = f32[2,2,256,256]{3,2,1,0:T(8,128)S(1)} copy-done((f32[2,2,256,256]{3,2,1,0:T(8,128)S(1)}, f32[2,2,256,256]{3,2,1,0:T(8,128)}, u32[]{:S(2)}) %copy-start.1) | copy-done | bytes 1048600
  2.7 0.0 copy-start.2
  2.7 0.0 copy-start.3
  2.7 13.2 %shard_map.68.ext = f32[2,2,328,384]{3,2,1,0:T(8,128)S(1)} custom-call(f32[2,2,256,256]{3,2,1,0:T(8,128)S(1)} %copy-done.1), custom_call_target="tpu_custom_call" | custom-call | tf_op jit(solution)/shard_map/pallas_call | solution.py:410
  15.9 0.0 copy-done
  16.0 0.0 copy-done.2
  16.0 0.0 copy-done.3
  16.0 16.6 %shard_map.69 = (f32[2,2,328,384]{3,2,1,0:T(8,128)S(1)}, f32[1024,128]{1,0:T(8,128)S(1)}) custom-call(s32[1,1,3,2]{3,2,1,0:T(4,128)S(1)} %copy.7.off_ref, f32[2,2,328,384]{3,2,1,0:T(8,128)S(1)} %shard_map.68.ext, f32[2,4,128,128]{3,2,1,0:T(8,128)S(1)} %copy-done, f32[1,1,3,128,128]{4,3,2,1,0:T(8,128)S(1)} %copy-done.3, bf16[8,256,256]{2,1,0:T(8,128)(2,1)S(1)} %copy-done.2), custom_call_target="tpu_custom_call" | custom-call | tf_op jit(solution)/shard_map/pallas_call | solution.py:427
  32.6 32.3 %shard_map.70 = (f32[2,2,256,256]{3,2,1,0:T(8,128)S(1)}, f32[2,4,128,128]{3,2,1,0:T(8,128)S(1)}) custom-call(f32[2,2,328,384]{3,2,1,0:T(8,128)S(1)} %get-tuple-element.4.acc, f32[1024,128]{1,0:T(8,128)S(1)} %get-tuple-element.5.gprobe, f32[2,4,128,128]{3,2,1,0:T(8,128)S(1)} %copy-done), custom_call_target="tpu_custom_call" | custom-call | tf_op jit(solution)/shard_map/pallas_call | solution.py:441
  65.0 1.0 %copy.10 = f32[2,2,256,256]{3,2,1,0:T(8,128)} copy(f32[2,2,256,256]{3,2,1,0:T(8,128)S(1)} %get-tuple-element.8) | data formatting | bytes 2097152
  65.9 0.8 %copy.11 = f32[2,4,128,128]{3,2,1,0:T(8,128)} copy(f32[2,4,128,128]{3,2,1,0:T(8,128)S(1)} %get-tuple-element.9) | data formatting | bytes 1048576
Async XLA Ops:
  0.6 15.3 %copy-start = (f32[2,4,128,128]{3,2,1,0:T(8,128)S(1)}, f32[2,4,128,128]{3,2,1,0:T(8,128)}, u32[]{:S(2)}) copy-start(f32[2,4,128,128]{3,2,1,0:T(8,128)} %probe_ref.3) | copy-start | bytes 1572868
  1.5 1.2 %copy-start.1 = (f32[2,2,256,256]{3,2,1,0:T(8,128)S(1)}, f32[2,2,256,256]{3,2,1,0:T(8,128)}, u32[]{:S(2)}) copy-start(f32[2,2,256,256]{3,2,1,0:T(8,128)} %obj_ref.1) | copy-start | bytes 3145732
  2.7 13.3 %copy-start.2 = (bf16[8,256,256]{2,1,0:T(8,128)(2,1)S(1)}, bf16[8,256,256]{2,1,0:T(8,128)(2,1)}, u32[]{:S(2)}) copy-start(bf16[8,256,256]{2,1,0:T(8,128)(2,1)} %constant.2.clone.tab) | copy-start | bytes 3145732
  2.7 13.3 %copy-start.3 = (f32[1,1,3,128,128]{4,3,2,1,0:T(8,128)S(1)}, f32[1,1,3,128,128]{4,3,2,1,0:T(8,128)}, u32[]{:S(2)}) copy-start(f32[1,1,3,128,128]{4,3,2,1,0:T(8,128)} %amp_ref.1) | copy-start | bytes 589828
where the time goes:
time: 67.3 us; the launch traced here: 66.7 us
  Pallas kernels  62.2 us (92%)
  local copies, waits for them, and re-layouts  3.82 us (6%)
  between operations  0.69 us (1%)
    pallas_call x1, Pallas kernels, on_device(): pl.pallas_call(functools.partial(sum_kernel, (n_row, n_col, chunks)), out...  32.3 us
    pallas_call x1, Pallas kernels, on_device(): pl.pallas_call(functools.partial(local_kernel, (win, scans)), out_shape=(...  16.6 us
    pallas_call x1, Pallas kernels, on_device(): pl.pallas_call(functools.partial(halo_kernel, (n_row, n_col)), out_shape=...  13.2 us
    unnamed x11, local copies, waits for them, and re-layouts  3.82 us

commit v1 on v0

--- a/solution.py
+++ b/solution.py
@@ -80,9 +80,9 @@
 EVERY = slice(None)
 
 
-def packed(get, first, rows):
+def packed(get, first, rows, count=4):
     out = None
-    for ch in range(4):
+    for ch in range(count):
         shift = (HALO * ch - first) % LANES
         block = get(ch)
         block = pltpu.roll(block, shift, 1) if shift else block
@@ -171,14 +171,9 @@
         ext[CHANS[ch] + (pl.ds(0, tall), pl.ds(tile, LANES))] = edge
 
 
-def local_kernel(
-    sizes, off_ref, ext, probe_ref, amp_ref, tab, acc, gprobe, winds, wave, far, factor, gobj
-):
+def window_kernel(sizes, off_ref, ext, winds):
     win, scans = sizes
     wide = ext.shape[3]
-    acc[...] = jnp.zeros_like(acc)
-    gprobe[...] = jnp.zeros_like(gprobe)
-    gobj[...] = jnp.zeros_like(gobj)
 
     @pl.loop(0, scans)
     def _(s):
@@ -186,12 +181,72 @@
         base = pl.multiple_of(row - lax.rem(row, SUB), SUB)
         rest = lax.rem(win + SUB - lax.rem(row, SUB), win + SUB)
         shift = lax.rem(wide + HALO - off_ref[0, 0, s, 1], wide)
-        o = {}
         for ch, (part, lay) in enumerate(CHANS):
             block = ext[part, lay, pl.ds(base, win + SUB), :]
             block = pltpu.roll(block, shift, 1)[:, :win]
-            o[part, lay] = pltpu.roll(block, rest, 0)[:win]
-            winds[s, ch] = o[part, lay]
+            winds[s, ch] = pltpu.roll(block, rest, 0)[:win]
+
+
+def main_kernel(
+    sizes,
+    off_ref,
+    winds,
+    probe_ref,
+    amp_ref,
+    tab,
+    grad_ref,
+    new_ref,
+    wave,
+    far,
+    factor,
+    gobj,
+    gprobe,
+    acc,
+    total,
+    spread,
+    from_top,
+    from_bot,
+    edge_l,
+    edge_r,
+    from_l,
+    from_r,
+    half_in,
+    half_sum,
+    parts,
+    g_send,
+    g_recv,
+    pair_send,
+    pair_recv,
+    rs_send,
+    rs_recv,
+    ag_send,
+    ag_recv,
+    fw_send,
+    fw_recv,
+):
+    n_row, n_col, win, scans, chunks = sizes
+    n_dev = n_row * n_col
+    n_half = n_col // 2
+    group = n_row * n_half
+    tile = grad_ref.shape[2]
+    tall, wide = tile + 2 * HALO, tile + LANES
+    my_r, my_c, up, down, lft, rgt = places(n_row, n_col)
+    head, tail, mid, after, body = zones(tile)
+    me = my_r * n_col + my_c
+    barrier = pltpu.get_barrier_semaphore()
+
+    @pl.loop(1, n_dev)
+    def _(k):
+        other = lax.rem(me + k, n_dev)
+        where = (other // n_col, lax.rem(other, n_col))
+        pl.semaphore_signal(barrier, inc=1, device_id=where, device_id_type=MESH)
+
+    gprobe[...] = jnp.zeros_like(gprobe)
+    gobj[...] = jnp.zeros_like(gobj)
+
+    @pl.loop(0, scans)
+    def _(s):
+        o = {chan: winds[s, ch] for ch, chan in enumerate(CHANS)}
         power = None
         for p in range(2):
             rows = []
@@ -220,19 +275,21 @@
         root = jnp.sqrt(power + SHIFT_AMP)
         factor[s] = 2.0 * (root - amp_ref[0, 0, s]) / root
 
-    def backward(p, s):
-        f = factor[s]
-        g = far[s, p] * twice(twice(f, 0), 1)
+
+    def first_half(p, s):
+        g = far[s, p] * twice(twice(factor[s], 0), 1)
         g = left(swap(right(g, tab, INV)), tab, INV)
         w = wave[s, p]
         gr, gi, wr, wi = g[:win], g[win:], w[:win], w[win:]
         re = wr * gr + wi * gi
         im = wr * gi - wi * gr
-        gobj[s, 1] += re[:, :win] + re[:, win:]
-        gobj[s, 3] += im[:, :win] + im[:, win:]
+        gobj[1, 0, s] += re[:, :win] + re[:, win:]
+        gobj[1, 1, s] += im[:, :win] + im[:, win:]
         o1r, o1i = twice(winds[s, 1], 1), twice(winds[s, 3], 1)
-        g = jnp.concatenate([o1r * gr + o1i * gi, o1r * gi - o1i * gr], axis=0)
-        g = right(swap(left(g, tab, KER_INV)), tab, KER_INV)
+        far[s, p] = jnp.concatenate([o1r * gr + o1i * gi, o1r * gi - o1i * gr], axis=0)
+
+    def second_half(p, s):
+        g = right(swap(left(far[s, p], tab, KER_INV)), tab, KER_INV)
         o0r, o0i = winds[s, 0], winds[s, 2]
         re = im = None
         for m in range(2):
@@ -244,141 +301,175 @@
             at = rows_of(p, win)
             gprobe[pl.ds(at[0][m], win)] += o0r * gr + o0i * gi
             gprobe[pl.ds(at[1][m], win)] += o0r * gi - o0i * gr
-        gobj[s, 0] += re
-        gobj[s, 2] += im
-
-    @pl.loop(0, scans)
-    def _(s):
-        backward(0, s)
-
-    @pl.loop(0, scans)
-    def _(s):
-        backward(1, s)
-        row = off_ref[0, 0, s, 0]
-        rest = lax.rem(row, SUB)
-        base = pl.multiple_of(row - rest, SUB)
-        shift = lax.rem(wide - HALO + off_ref[0, 0, s, 1], wide)
-        for ch, (part, lay) in enumerate(CHANS):
-            block = jnp.concatenate([gobj[s, ch], jnp.zeros((SUB, win), F32)], axis=0)
-            block = pltpu.roll(block, rest, 0)
-            block = jnp.concatenate([block, jnp.zeros((win + SUB, wide - win), F32)], axis=1)
-            acc[part, lay, pl.ds(base, win + SUB), :] += pltpu.roll(block, shift, 1)
-
-
-def sum_kernel(
-    sizes,
-    acc,
-    gprobe,
-    probe_ref,
-    grad_ref,
-    new_ref,
-    total,
-    from_top,
-    from_bot,
-    edge_l,
-    edge_r,
-    from_l,
-    from_r,
-    parts,
-    g_send,
-    g_recv,
-    rs_send,
-    rs_recv,
-    ag_send,
-    ag_recv,
-):
-    n_row, n_col, chunks = sizes
-    n_dev = n_row * n_col
-    tile, win = grad_ref.shape[2], probe_ref.shape[2]
-    tall = tile + 2 * HALO
-    my_r, my_c, up, down, lft, rgt = places(n_row, n_col)
-    head, tail, mid, after, body = zones(tile)
-    me = my_r * n_col + my_c
-
-    def peer(k):
-        other = lax.rem(me + k, n_dev)
-        return other, (other // n_col, lax.rem(other, n_col))
-
-    barrier = pltpu.get_barrier_semaphore()
-
-    @pl.loop(1, n_dev)
-    def _(k):
-        pl.semaphore_signal(barrier, inc=1, device_id=peer(k)[1], device_id_type=MESH)
-
-    tall_rows = pl.ds(0, tall)
-    edge_of = lambda ch: acc[CHANS[ch] + (tall_rows, pl.ds(tile, LANES))]
-    edge_r[...] = packed(edge_of, 0, tall)
-    edge_l[...] = packed(edge_of, LANES - HALO, tall)
-    pl.semaphore_wait(barrier, n_dev - 1)
+        gobj[0, 0, s] += re
+        gobj[0, 1, s] += im
+
+    def one_hot(at, target):
+        return jnp.where(at == target, 1.0, 0.0).astype(BF16)
+
+    def place(lay):
+        for s in range(scans):
+            k = lax.broadcasted_iota(jnp.int32, (win, wide), 0) + (off_ref[0, 0, s, 1] - HALO)
+            k = jnp.where(k < 0, k + wide, k)
+            cols = one_hot(lax.broadcasted_iota(jnp.int32, (win, wide), 1), k)
+            for part in range(2):
+                for t, term in enumerate(split(gobj[lay, part, s])):
+                    spread[t, pl.ds(s * win, win), pl.ds(part * wide, wide)] = dot(
+                        term, cols
+                    ).astype(BF16)
+        rows = []
+        for s in range(scans):
+            j = lax.broadcasted_iota(jnp.int32, (tall, win), 1) + off_ref[0, 0, s, 0]
+            rows.append(one_hot(lax.broadcasted_iota(jnp.int32, (tall, win), 0), j))
+        rows = jnp.concatenate(rows, axis=1)
+        for part in range(2):
+            cut = pl.ds(part * wide, wide)
+            acc[part, lay] = dot(rows, spread[0, :, cut]) + dot(rows, spread[1, :, cut])
+
+    def grads_start(lay):
+        edge_of = lambda ch: acc[ch, lay, :, pl.ds(tile, LANES)]
+        er, el, fl, fr = edge_r.at[lay], edge_l.at[lay], from_l.at[lay], from_r.at[lay]
+        er[...] = packed(edge_of, 0, tall, 2)
+        el[...] = packed(edge_of, LANES - HALO, tall, 2)
+        ss, rs = g_send.at[lay], g_recv.at[lay]
+        return [
+            send(acc.at[:, lay, head, body], from_bot.at[lay], ss, rs, 0, (up, my_c)),
+            send(acc.at[:, lay, after, body], from_top.at[lay], ss, rs, 1, (down, my_c)),
+            send(er.at[mid], fl.at[mid], ss, rs, 2, (my_r, rgt)),
+            send(el.at[mid], fr.at[mid], ss, rs, 3, (my_r, lft)),
+            send(er.at[head], fl.at[after], ss, rs, 4, (up, rgt)),
+            send(er.at[after], fl.at[head], ss, rs, 5, (down, rgt)),
+            send(el.at[head], fr.at[after], ss, rs, 6, (up, lft)),
+            send(el.at[after], fr.at[head], ss, rs, 7, (down, lft)),
+        ]
+
+    def grads_end(lay, copies):
+        grad_ref[:, lay] = acc[:, lay, mid, body]
+        for copy in copies:
+            copy.wait()
+        grad_ref[:, lay, head, :] += from_top[lay]
+        grad_ref[:, lay, tail, :] += from_bot[lay]
+        for ref, first, cols in (
+            (from_l, 0, pl.ds(0, LANES)),
+            (from_r, LANES - HALO, pl.ds(tile - LANES, LANES)),
+        ):
+            for ch in range(2):
+                at = lane(tall)
+                block = unpacked(ref[lay], ch, first)
+                block = jnp.where((at >= first) & (at < first + HALO), block, 0.0)
+                grad_ref[ch, lay, :, cols] += block[HALO : HALO + tile]
+                grad_ref[ch, lay, head, cols] += block[:HALO]
+                grad_ref[ch, lay, tail, cols] += block[HALO + tile :]
 
     n_rows = gprobe.shape[0] // chunks
-    piece = n_rows // n_dev
-
-    def scatter_start(c):
-        @pl.loop(1, n_dev)
+    half = n_rows // 2
+    piece = half // group
+    odd = lax.rem(my_c, 2)
+    partner = (my_r, my_c + 1 - 2 * odd)
+    place_in = my_r * n_half + my_c // 2
+
+    def mate(k):
+        other = lax.rem(place_in + k, group)
+        return other, (other // n_half, 2 * lax.rem(other, n_half) + odd)
+
+    def rows_at(start, size):
+        return pl.ds(pl.multiple_of(start, piece), size)
+
+    def wait_all(sem, ref):
+        pltpu.make_async_copy(ref, ref, sem).wait()
+
+    def owned(c, q):
+        return rows_at(c * n_rows + odd * half + q * piece, piece)
+
+    def pair_start(c):
+        return send(
+            gprobe.at[rows_at(c * n_rows + (1 - odd) * half, half)],
+            half_in.at[c],
+            pair_send,
+            pair_recv,
+            c,
+            partner,
+        )
+
+    def scatter_start(c, copy):
+        copy.wait()
+        half_sum[c] = gprobe[rows_at(c * n_rows + odd * half, half)] + half_in[c]
+
+        @pl.loop(1, group)
         def _(k):
-            other, where = peer(k)
+            other, where = mate(k)
             send(
-                gprobe.at[pl.ds(pl.multiple_of(c * n_rows + other * piece, piece), piece)],
-                parts.at[c, pl.ds(pl.multiple_of((k - 1) * piece, piece), piece)],
+                half_sum.at[c, rows_at(other * piece, piece)],
+                parts.at[c, rows_at((k - 1) * piece, piece)],
                 rs_send,
                 rs_recv,
                 c,
                 where,
             )
 
-    mine = [
-        pl.ds(pl.multiple_of(c * n_rows + me * piece, piece), piece) for c in range(chunks)
-    ]
-
-    def wait_all(sem, ref):
-        pltpu.make_async_copy(ref, ref, sem).wait()
-
     def gather_start(c):
         wait_all(rs_recv.at[c], parts.at[c])
-        value = gprobe[mine[c]]
-        for k in range(n_dev - 1):
+        value = half_sum[c, rows_at(place_in * piece, piece)]
+        for k in range(group - 1):
             value = value + parts[c, pl.ds(k * piece, piece)]
-        total[mine[c]] = value
-
-        @pl.loop(1, n_dev)
+        own = owned(c, place_in)
+        total[own] = value
+
+        @pl.loop(1, group)
         def _(k):
-            _, where = peer(k)
-            send(total.at[mine[c]], total.at[mine[c]], ag_send, ag_recv, c, where)
-
+            pltpu.make_async_remote_copy(
+                src_ref=total.at[own],
+                dst_ref=total.at[own],
+                send_sem=ag_send.at[c],
+                recv_sem=ag_recv.at[c, k],
+                device_id=mate(k)[1],
+                device_id_type=MESH,
+            ).start()
+
+        send(total.at[own], total.at[own], fw_send, fw_recv, c, partner)
+
+    def forward_start(c):
+        @pl.loop(1, group)
+        def _(k):
+            got = total.at[owned(c, lax.rem(place_in + group - k, group))]
+            wait_all(ag_recv.at[c, k], got)
+            send(got, got, fw_send, fw_recv, c, partner)
+
+    for p in range(2):
+
+        @pl.loop(0, scans)
+        def _(s):
+            first_half(p, s)
+
+    place(1)
+    pl.semaphore_wait(barrier, n_dev - 1)
+    copies_1 = grads_start(1)
+
+    @pl.loop(0, scans)
+    def _(s):
+        second_half(0, s)
+
+    early = chunks == 2
+    pair_copy = pair_start(0) if early else None
+    for s in range(scans):
+        second_half(1, s)
+        if early and s == 0:
+            scatter_start(0, pair_copy)
+        if early and s == scans - 1:
+            gather_start(0)
+    late = chunks - 1
+    pair_copy = pair_start(late)
+    place(0)
+    copies_0 = grads_start(0)
+    scatter_start(late, pair_copy)
+    if early:
+        forward_start(0)
+    grads_end(1, copies_1)
+    gather_start(late)
+    grads_end(0, copies_0)
+    forward_start(late)
     for c in range(chunks):
-        scatter_start(c)
-    grads = [
-        send(acc.at[:, :, head, body], from_bot, g_send, g_recv, 0, (up, my_c)),
-        send(acc.at[:, :, after, body], from_top, g_send, g_recv, 1, (down, my_c)),
-        send(edge_r.at[mid], from_l.at[mid], g_send, g_recv, 2, (my_r, rgt)),
-        send(edge_l.at[mid], from_r.at[mid], g_send, g_recv, 3, (my_r, lft)),
-        send(edge_r.at[head], from_l.at[after], g_send, g_recv, 4, (up, rgt)),
-        send(edge_r.at[after], from_l.at[head], g_send, g_recv, 5, (down, rgt)),
-        send(edge_l.at[head], from_r.at[after], g_send, g_recv, 6, (up, lft)),
-        send(edge_l.at[after], from_r.at[head], g_send, g_recv, 7, (down, lft)),
-    ]
-    for c in range(chunks):
-        gather_start(c)
-    grad_ref[...] = acc[:, :, mid, body]
-    for copy in grads:
-        copy.wait()
-    grad_ref[:, :, head, :] += from_top[...]
-    grad_ref[:, :, tail, :] += from_bot[...]
-    for ref, first, cols in (
-        (from_l, 0, pl.ds(0, LANES)),
-        (from_r, LANES - HALO, pl.ds(tile - LANES, LANES)),
-    ):
-        for ch in range(4):
-            at = lane(tall)
-            block = unpacked(ref[...], ch, first)
-            block = jnp.where((at >= first) & (at < first + HALO), block, 0.0)
-            part, lay = CHANS[ch]
-            grad_ref[part, lay, :, cols] += block[HALO : HALO + tile]
-            grad_ref[part, lay, head, cols] += block[:HALO]
-            grad_ref[part, lay, tail, cols] += block[HALO + tile :]
-    for c in range(chunks):
-        wait_all(ag_recv.at[c], parts.at[c])
+        wait_all(fw_recv.at[c], half_in.at[c])
     full = total[...]
     scale = STEP_SIZE / jnp.sqrt(jnp.sum(full * full, keepdims=True) / full.size + EPSILON)
     for p in range(2):
@@ -391,6 +482,7 @@
     for c in range(chunks):
         wait_all(rs_send.at[c], parts.at[c])
         wait_all(ag_send.at[c], parts.at[c])
+        wait_all(fw_send.at[c], half_in.at[c])
 
 
 def on_device(object_tiles, probe_modes, offsets, amplitude):
@@ -400,11 +492,13 @@
     tall, wide = tile + 2 * HALO, tile + LANES
     g_rows = 2 * probe_modes.shape[1] * win
     chunks = 2 if g_rows // 2 % (8 * n_dev) == 0 else 1
-    piece = g_rows // chunks // n_dev
+    half = g_rows // chunks // 2
+    group = n_dev // 2
     vmem = pl.BlockSpec(memory_space=pltpu.VMEM)
     smem = pl.BlockSpec(memory_space=pltpu.SMEM)
     dma = pltpu.SemaphoreType.DMA
     side = pltpu.VMEM((tall, LANES), F32)
+    sides = pltpu.VMEM((2, tall, LANES), F32)
     wide_tile = jax.ShapeDtypeStruct((2, 2, tall + SUB, wide), F32)
     limit = 40 * 1024 * 1024
     ext = pl.pallas_call(
@@ -424,48 +518,54 @@
             collective_id=0, has_side_effects=True, vmem_limit_bytes=limit
         ),
     )(object_tiles)
-    acc, gprobe = pl.pallas_call(
-        functools.partial(local_kernel, (win, scans)),
-        out_shape=(wide_tile, jax.ShapeDtypeStruct((g_rows, win), F32)),
-        in_specs=[smem] + [vmem] * 4,
-        out_specs=(vmem, vmem),
-        scratch_shapes=[
-            pltpu.VMEM((scans, 4, win, win), F32),
-            pltpu.VMEM((scans, 2, 2 * win, 2 * win), F32),
-            pltpu.VMEM((scans, 2, 2 * win, 2 * win), F32),
-            pltpu.VMEM((scans, win, win), F32),
-            pltpu.VMEM((scans, 4, win, win), F32),
-        ],
+    winds = pl.pallas_call(
+        functools.partial(window_kernel, (win, scans)),
+        out_shape=jax.ShapeDtypeStruct((scans, 4, win, win), F32),
+        in_specs=[smem, vmem],
+        out_specs=vmem,
         compiler_params=pltpu.CompilerParams(vmem_limit_bytes=limit),
-    )(offsets, ext, probe_modes, amplitude, jnp.asarray(tables(win)))
+    )(offsets, ext)
     return pl.pallas_call(
-        functools.partial(sum_kernel, (n_row, n_col, chunks)),
+        functools.partial(main_kernel, (n_row, n_col, win, scans, chunks)),
         out_shape=(
             jax.ShapeDtypeStruct(object_tiles.shape, F32),
             jax.ShapeDtypeStruct(probe_modes.shape, F32),
         ),
-        in_specs=[vmem] * 3,
+        in_specs=[smem] + [vmem] * 4,
         out_specs=(vmem, vmem),
         scratch_shapes=[
+            pltpu.VMEM((scans, 2, 2 * win, 2 * win), F32),
+            pltpu.VMEM((scans, 2, 2 * win, 2 * win), F32),
+            pltpu.VMEM((scans, win, win), F32),
+            pltpu.VMEM((2, 2, scans, win, win), F32),
             pltpu.VMEM((g_rows, win), F32),
+            pltpu.VMEM((2, 2, tall, wide), F32),
+            pltpu.VMEM((g_rows, win), F32),
+            pltpu.VMEM((2, scans * win, 2 * wide), BF16),
             pltpu.VMEM((2, 2, HALO, tile), F32),
             pltpu.VMEM((2, 2, HALO, tile), F32),
-            side,
-            side,
-            side,
-            side,
-            pltpu.VMEM((chunks, (n_dev - 1) * piece, win), F32),
-            dma((8,)),
-            dma((8,)),
-            dma((chunks,)),
-            dma((chunks,)),
+            sides,
+            sides,
+            sides,
+            sides,
+            pltpu.VMEM((chunks, half, win), F32),
+            pltpu.VMEM((chunks, half, win), F32),
+            pltpu.VMEM((chunks, half - half // group, win), F32),
+            dma((2, 8)),
+            dma((2, 8)),
+            dma((chunks,)),
+            dma((chunks,)),
+            dma((chunks,)),
+            dma((chunks,)),
+            dma((chunks,)),
+            dma((chunks, group)),
             dma((chunks,)),
             dma((chunks,)),
         ],
         compiler_params=pltpu.CompilerParams(
             collective_id=1, has_side_effects=True, vmem_limit_bytes=limit
         ),
-    )(acc, gprobe, probe_modes)
+    )(offsets, winds, probe_modes, amplitude, jnp.asarray(tables(win)))
 
 
 def solution(mesh):

time: 67.3 us -> 62.4 us (0.927)
  Pallas kernels: 62.2 us -> 57.8 us
    pallas_call x2, Pallas kernels: 49 us -> 44.5 us  [the longest x1 43 us: on_device(): pl.pallas_call(functools.partial(main_kernel, (n_row, n_col, win, scans,...]
where the time goes in v1:
time: 62.4 us; the launch traced here: 62.2 us
  Pallas kernels  57.8 us (93%)
  local copies, waits for them, and re-layouts  3.77 us (6%)
  between operations  0.7 us (1%)
    pallas_call x1, Pallas kernels, on_device(): pl.pallas_call(functools.partial(main_kernel, (n_row, n_col, win, scans,...  43 us
    pallas_call x1, Pallas kernels, on_device(): pl.pallas_call(functools.partial(halo_kernel, (n_row, n_col)), out_shape=...  13.2 us
    unnamed x11, local copies, waits for them, and re-layouts  3.77 us
    pallas_call x1, Pallas kernels, on_device(): pl.pallas_call(functools.partial(window_kernel, (win, scans)), out_shape=...  1.5 us

profile of v1, /device:TPU:1, one launch (start us, length us, event | category | flops | bytes accessed | tf_op | source)
XLA Modules:
  0.0 62.2 jit_solution(10010884668212886020)
XLA Ops:
  0.6 0.8 %copy.8.off_ref = s32[1,1,3,2]{3,2,1,0:T(4,128)S(1)} copy(s32[1,1,3,2]{2,3,1,0:T(2,128)} %param.7) | data formatting | bytes 48 | tf_op args[2]
  1.4 0.0 copy-start
  1.4 1.2 %copy-done = f32[2,2,256,256]{3,2,1,0:T(8,128)S(1)} copy-done((f32[2,2,256,256]{3,2,1,0:T(8,128)S(1)}, f32[2,2,256,256]{3,2,1,0:T(8,128)}, u32[]{:S(2)}) %copy-start) | copy-done | bytes 1048600
  2.6 13.2 %shard_map.68.ext = f32[2,2,328,384]{3,2,1,0:T(8,128)S(1)} custom-call(f32[2,2,256,256]{3,2,1,0:T(8,128)S(1)} %copy-done), custom_call_target="tpu_custom_call" | custom-call | tf_op jit(solution)/shard_map/pallas_call | solution.py:504
  15.9 0.0 copy-start.1
  15.9 0.0 copy-start.2
  15.9 0.0 copy-start.3
  15.9 1.5 %shard_map.69.winds = f32[3,4,128,128]{3,2,1,0:T(8,128)S(1)} custom-call(s32[1,1,3,2]{3,2,1,0:T(4,128)S(1)} %copy.8.off_ref, f32[2,2,328,384]{3,2,1,0:T(8,128)S(1)} %shard_map.68.ext), custom_call_target="tpu_custom_call" | custom-call | tf_op jit(solution)/shard_map/pallas_call | solution.py:521
  17.4 0.0 copy-done.1
  17.4 0.0 copy-done.2
  17.4 0.0 copy-done.3
  17.5 43.0 %shard_map.70 = (f32[2,2,256,256]{3,2,1,0:T(8,128)S(1)}, f32[2,4,128,128]{3,2,1,0:T(8,128)S(1)}) custom-call(s32[1,1,3,2]{3,2,1,0:T(4,128)S(1)} %copy.8.off_ref, f32[3,4,128,128]{3,2,1,0:T(8,128)S(1)} %shard_map.69.winds, f32[2,4,128,128]{3,2,1,0:T(8,128)S(1)} %copy-done.2, f32[1,1,3,128,128]{4,3,2,1,0:T(8,128)S(1)} %copy-done.3, ...), custom_call_target="tpu_custom_call" | custom-call | tf_op jit(solution)/shard_map/pallas_call | solution.py:528
  60.5 1.0 %copy.11 = f32[2,2,256,256]{3,2,1,0:T(8,128)} copy(f32[2,2,256,256]{3,2,1,0:T(8,128)S(1)} %get-tuple-element.4) | data formatting | bytes 2097152
  61.4 0.8 %copy.12 = f32[2,4,128,128]{3,2,1,0:T(8,128)} copy(f32[2,4,128,128]{3,2,1,0:T(8,128)S(1)} %get-tuple-element.5) | data formatting | bytes 1048576
Async XLA Ops:
  1.4 1.2 %copy-start = (f32[2,2,256,256]{3,2,1,0:T(8,128)S(1)}, f32[2,2,256,256]{3,2,1,0:T(8,128)}, u32[]{:S(2)}) copy-start(f32[2,2,256,256]{3,2,1,0:T(8,128)} %obj_ref.1) | copy-start | bytes 3145732
  15.9 1.5 %copy-start.1 = (bf16[8,256,256]{2,1,0:T(8,128)(2,1)S(1)}, bf16[8,256,256]{2,1,0:T(8,128)(2,1)}, u32[]{:S(2)}) copy-start(bf16[8,256,256]{2,1,0:T(8,128)(2,1)} %constant.2.clone.tab) | copy-start | bytes 3145732
  15.9 1.5 %copy-start.2 = (f32[2,4,128,128]{3,2,1,0:T(8,128)S(1)}, f32[2,4,128,128]{3,2,1,0:T(8,128)}, u32[]{:S(2)}) copy-start(f32[2,4,128,128]{3,2,1,0:T(8,128)} %probe_ref.1) | copy-start | bytes 1572868
  15.9 1.5 %copy-start.3 = (f32[1,1,3,128,128]{4,3,2,1,0:T(8,128)S(1)}, f32[1,1,3,128,128]{4,3,2,1,0:T(8,128)}, u32[]{:S(2)}) copy-start(f32[1,1,3,128,128]{4,3,2,1,0:T(8,128)} %amp_ref.1) | copy-start | bytes 589828

commit v2 on v1

--- a/solution.py
+++ b/solution.py
@@ -177,10 +177,10 @@
 
     @pl.loop(0, scans)
     def _(s):
-        row = off_ref[0, 0, s, 0]
+        row = off_ref[0, 0, 0, s]
         base = pl.multiple_of(row - lax.rem(row, SUB), SUB)
         rest = lax.rem(win + SUB - lax.rem(row, SUB), win + SUB)
-        shift = lax.rem(wide + HALO - off_ref[0, 0, s, 1], wide)
+        shift = lax.rem(wide + HALO - off_ref[0, 0, 1, s], wide)
         for ch, (part, lay) in enumerate(CHANS):
             block = ext[part, lay, pl.ds(base, win + SUB), :]
             block = pltpu.roll(block, shift, 1)[:, :win]
@@ -309,7 +309,7 @@
 
     def place(lay):
         for s in range(scans):
-            k = lax.broadcasted_iota(jnp.int32, (win, wide), 0) + (off_ref[0, 0, s, 1] - HALO)
+            k = lax.broadcasted_iota(jnp.int32, (win, wide), 0) + (off_ref[0, 0, 1, s] - HALO)
             k = jnp.where(k < 0, k + wide, k)
             cols = one_hot(lax.broadcasted_iota(jnp.int32, (win, wide), 1), k)
             for part in range(2):
@@ -319,7 +319,7 @@
                     ).astype(BF16)
         rows = []
         for s in range(scans):
-            j = lax.broadcasted_iota(jnp.int32, (tall, win), 1) + off_ref[0, 0, s, 0]
+            j = lax.broadcasted_iota(jnp.int32, (tall, win), 1) + off_ref[0, 0, 0, s]
             rows.append(one_hot(lax.broadcasted_iota(jnp.int32, (tall, win), 0), j))
         rows = jnp.concatenate(rows, axis=1)
         for part in range(2):
@@ -435,37 +435,40 @@
             wait_all(ag_recv.at[c, k], got)
             send(got, got, fw_send, fw_recv, c, partner)
 
-    for p in range(2):
-
-        @pl.loop(0, scans)
-        def _(s):
-            first_half(p, s)
-
-    place(1)
-    pl.semaphore_wait(barrier, n_dev - 1)
-    copies_1 = grads_start(1)
+    early = chunks == 2
+    late = chunks - 1
 
     @pl.loop(0, scans)
     def _(s):
+        first_half(0, s)
         second_half(0, s)
 
-    early = chunks == 2
-    pair_copy = pair_start(0) if early else None
-    for s in range(scans):
+    pl.semaphore_wait(barrier, n_dev - 1)
+    pair_0 = pair_start(0) if early else None
+
+    @pl.loop(0, scans)
+    def _(s):
+        first_half(1, s)
+
+    if early:
+        scatter_start(0, pair_0)
+    place(1)
+    copies_1 = grads_start(1)
+
+    @pl.loop(0, scans)
+    def _(s):
         second_half(1, s)
-        if early and s == 0:
-            scatter_start(0, pair_copy)
-        if early and s == scans - 1:
-            gather_start(0)
-    late = chunks - 1
-    pair_copy = pair_start(late)
+
+    pair_1 = pair_start(late)
     place(0)
+    scatter_start(late, pair_1)
+    if early:
+        gather_start(0)
     copies_0 = grads_start(0)
-    scatter_start(late, pair_copy)
+    grads_end(1, copies_1)
+    gather_start(late)
     if early:
         forward_start(0)
-    grads_end(1, copies_1)
-    gather_start(late)
     grads_end(0, copies_0)
     forward_start(late)
     for c in range(chunks):
@@ -501,6 +504,7 @@
     sides = pltpu.VMEM((2, tall, LANES), F32)
     wide_tile = jax.ShapeDtypeStruct((2, 2, tall + SUB, wide), F32)
     limit = 40 * 1024 * 1024
+    pairs = offsets.transpose(0, 1, 3, 2)
     ext = pl.pallas_call(
         functools.partial(halo_kernel, (n_row, n_col)),
         out_shape=wide_tile,
@@ -524,7 +528,7 @@
         in_specs=[smem, vmem],
         out_specs=vmem,
         compiler_params=pltpu.CompilerParams(vmem_limit_bytes=limit),
-    )(offsets, ext)
+    )(pairs, ext)
     return pl.pallas_call(
         functools.partial(main_kernel, (n_row, n_col, win, scans, chunks)),
         out_shape=(
@@ -565,7 +569,7 @@
         compiler_params=pltpu.CompilerParams(
             collective_id=1, has_side_effects=True, vmem_limit_bytes=limit
         ),
-    )(offsets, winds, probe_modes, amplitude, jnp.asarray(tables(win)))
+    )(pairs, winds, probe_modes, amplitude, jnp.asarray(tables(win)))
 
 
 def solution(mesh):

time: 62.4 us -> 57.6 us (0.923)
  Pallas kernels: 57.8 us -> 53.7 us
  local copies, waits for them, and re-layouts: 3.77 us -> 3.01 us
    pallas_call x1, Pallas kernels: 43 us -> 39 us  [on_device(): pl.pallas_call(functools.partial(main_kernel, (n_row, n_col, win, scans,...]
    unnamed x11 -> x12, local copies, waits for them, and re-layouts: 3.77 us -> 3.01 us
where the time goes in v2:
time: 57.6 us; the launch traced here: 57.5 us
  Pallas kernels  53.7 us (93%)
  local copies, waits for them, and re-layouts  3.01 us (5%)
  between operations  0.73 us (1%)
    pallas_call x1, Pallas kernels, on_device(): pl.pallas_call(functools.partial(main_kernel, (n_row, n_col, win, scans,...  39 us
    pallas_call x1, Pallas kernels, on_device(): pl.pallas_call(functools.partial(halo_kernel, (n_row, n_col)), out_shape=...  13.2 us
    unnamed x12, local copies, waits for them, and re-layouts  3.01 us
    pallas_call x1, Pallas kernels, on_device(): pl.pallas_call(functools.partial(window_kernel, (win, scans)), out_shape=...  1.48 us

profile of v2, /device:TPU:1, one launch (start us, length us, event | category | flops | bytes accessed | tf_op | source)
XLA Modules:
  0.0 57.5 jit_solution(2343200479184111821)
XLA Ops:
  0.6 0.0 copy-start.4
  0.6 0.0 copy-start
  0.6 1.2 %copy-done = f32[2,2,256,256]{3,2,1,0:T(8,128)S(1)} copy-done((f32[2,2,256,256]{3,2,1,0:T(8,128)S(1)}, f32[2,2,256,256]{3,2,1,0:T(8,128)}, u32[]{:S(2)}) %copy-start) | copy-done | bytes 1048600
  1.9 13.2 %shard_map.68.ext = f32[2,2,328,384]{3,2,1,0:T(8,128)S(1)} custom-call(f32[2,2,256,256]{3,2,1,0:T(8,128)S(1)} %copy-done), custom_call_target="tpu_custom_call" | custom-call | tf_op jit(solution)/shard_map/pallas_call | solution.py:508
  15.1 0.0 copy-done.4
  15.1 0.0 copy-start.1
  15.2 0.0 copy-start.2
  15.2 0.0 copy-start.3
  15.2 1.5 %shard_map.69.winds = f32[3,4,128,128]{3,2,1,0:T(8,128)S(1)} custom-call(s32[1,1,2,3]{3,2,1,0:T(2,128)S(1)} %bitcast.1, f32[2,2,328,384]{3,2,1,0:T(8,128)S(1)} %shard_map.68.ext), custom_call_target="tpu_custom_call" | custom-call | tf_op jit(solution)/shard_map/pallas_call | solution.py:525
  16.7 0.0 copy-done.1
  16.7 0.0 copy-done.2
  16.7 0.0 copy-done.3
  16.7 39.0 %shard_map.70 = (f32[2,2,256,256]{3,2,1,0:T(8,128)S(1)}, f32[2,4,128,128]{3,2,1,0:T(8,128)S(1)}) custom-call(s32[1,1,2,3]{3,2,1,0:T(2,128)S(1)} %bitcast.2, f32[3,4,128,128]{3,2,1,0:T(8,128)S(1)} %shard_map.69.winds, f32[2,4,128,128]{3,2,1,0:T(8,128)S(1)} %copy-done.2, f32[1,1,3,128,128]{4,3,2,1,0:T(8,128)S(1)} %copy-done.3, bf16[8,256,256]{2,1,0:T(8,128)(2,1)S(1)} %copy-done.1), custom_call_target="tpu_custom_call" | custom-call | tf_op jit(solution)/shard_map/pallas_call | solution.py:532
  55.7 1.0 %copy.9 = f32[2,2,256,256]{3,2,1,0:T(8,128)} copy(f32[2,2,256,256]{3,2,1,0:T(8,128)S(1)} %get-tuple-element.4) | data formatting | bytes 2097152
  56.7 0.8 %copy.10 = f32[2,4,128,128]{3,2,1,0:T(8,128)} copy(f32[2,4,128,128]{3,2,1,0:T(8,128)S(1)} %get-tuple-element.5) | data formatting | bytes 1048576
Async XLA Ops:
  0.6 14.5 %copy-start.4 = (s32[1,1,3,2]{2,3,1,0:T(2,128)S(1)}, s32[1,1,3,2]{2,3,1,0:T(2,128)}, u32[]{:S(2)}) copy-start(s32[1,1,3,2]{2,3,1,0:T(2,128)} %param.7) | copy-start | bytes 76
  0.6 1.2 %copy-start = (f32[2,2,256,256]{3,2,1,0:T(8,128)S(1)}, f32[2,2,256,256]{3,2,1,0:T(8,128)}, u32[]{:S(2)}) copy-start(f32[2,2,256,256]{3,2,1,0:T(8,128)} %obj_ref.1) | copy-start | bytes 3145732
  15.1 1.5 %copy-start.1 = (bf16[8,256,256]{2,1,0:T(8,128)(2,1)S(1)}, bf16[8,256,256]{2,1,0:T(8,128)(2,1)}, u32[]{:S(2)}) copy-start(bf16[8,256,256]{2,1,0:T(8,128)(2,1)} %constant.2.clone.tab) | copy-start | bytes 3145732
  15.2 1.5 %copy-start.2 = (f32[2,4,128,128]{3,2,1,0:T(8,128)S(1)}, f32[2,4,128,128]{3,2,1,0:T(8,128)}, u32[]{:S(2)}) copy-start(f32[2,4,128,128]{3,2,1,0:T(8,128)} %probe_ref.1) | copy-start | bytes 1572868
  15.2 1.5 %copy-start.3 = (f32[1,1,3,128,128]{4,3,2,1,0:T(8,128)S(1)}, f32[1,1,3,128,128]{4,3,2,1,0:T(8,128)}, u32[]{:S(2)}) copy-start(f32[1,1,3,128,128]{4,3,2,1,0:T(8,128)} %amp_ref.1) | copy-start | bytes 589828
